TPU v7x, 32 devices: a whole 2x2x4 slice. The times are simulated.
32 devices in a mesh: dp: 8 (over z, x), bn: 4 (over y, core).
Axes of the slice: x: 2, y: 2, z: 4, core: 2. Of those that a mesh axis runs over, the one named last changes fastest.
Arguments:
- features: bfloat16 [128, 19, 19, 1024], P(('dp', 'bn')), may hold values from -8 to 8
- image_counts: int32 [32], P(('dp', 'bn')), may hold values from 2 to 4, as said below
- map_sides: int32 [128], P(('dp', 'bn')), may hold values from 13 to 19, as said below
- split_kernel: bfloat16 [1024, 1024], replicated, may hold values from -0.1875 to 0.1875
- split_gain: float32 [1024], replicated, may hold values from 0.5 to 1.5
- split_shift: float32 [1024], replicated, may hold values from -2 to 2
- inner_kernel: bfloat16 [512, 512], replicated, may hold values from -0.25 to 0.25
- inner_gain: float32 [512], replicated, may hold values from 0.5 to 1.5
- inner_shift: float32 [512], replicated, may hold values from -2 to 2
- spread_kernel: bfloat16 [3, 3, 512, 512], replicated, may hold values from -0.09375 to 0.09375
- spread_gain: float32 [512], replicated, may hold values from 0.5 to 1.5
- spread_shift: float32 [512], replicated, may hold values from -2 to 2
- transition_kernel: bfloat16 [512, 512], replicated, may hold values from -0.25 to 0.25
- transition_gain: float32 [512], replicated, may hold values from 0.5 to 1.5
- transition_shift: float32 [512], replicated, may hold values from -2 to 2
- output_kernel: bfloat16 [1024, 1024], replicated, may hold values from -0.1875 to 0.1875
- output_gain: float32 [1024], replicated, may hold values from 0.5 to 1.5
- output_shift: float32 [1024], replicated, may hold values from -2 to 2
- cotangent: float32 [128, 19, 19, 1024], P(('dp', 'bn')), may hold values from -6 to 6
Outputs:
- result_map: float32 [128, 19, 19, 1024], P(('dp', 'bn'))
- grad_features: float32 [128, 19, 19, 1024], P(('dp', 'bn'))
- grad_split_kernel: float32 [1024, 1024], replicated
- grad_split_gain: float32 [1024], replicated
- grad_split_shift: float32 [1024], replicated
- grad_inner_kernel: float32 [512, 512], replicated
- grad_inner_gain: float32 [512], replicated
- grad_inner_shift: float32 [512], replicated
- grad_spread_kernel: float32 [3, 3, 512, 512], replicated
- grad_spread_gain: float32 [512], replicated
- grad_spread_shift: float32 [512], replicated
- grad_transition_kernel: float32 [512, 512], replicated
- grad_transition_gain: float32 [512], replicated
- grad_transition_shift: float32 [512], replicated
- grad_output_kernel: float32 [1024, 1024], replicated
- grad_output_gain: float32 [1024], replicated
- grad_output_shift: float32 [1024], replicated
Inputs may be any that keep to these rules, and one draw needn't show every extreme that they name: `image_counts`: each device has at least 2 live slots; some device has all 4. `map_sides`: each slot's side is 19, 16 or 13; sides of slots that are not live are to be ignored.
All inputs are finite; a program needn't handle non-finite values.
Results may differ from a plain program's by a relative error of at most 0.0003.
Values sent between devices are 32-bit elements; how exact they have to be, the bound alone decides.
A program may use at most 192 MiB of HBM per device.

v0:
```python
import jax
import jax.numpy as jnp
from jax import lax
from jax.sharding import PartitionSpec as P

SLOTS = 4
MAP = 19
epsilon = 1e-05


def mish(value):
    return value * jnp.tanh(jax.nn.softplus(value))


def convolve(inputs, kernel):
    return lax.conv_general_dilated(
        inputs,
        kernel,
        (1, 1),
        ((1, 1), (1, 1)),
        dimension_numbers=("NHWC", "HWIO", "NHWC"),
        precision=lax.Precision.HIGHEST,
    )


def pointwise(inputs, kernel):
    return jnp.einsum("nhwc,cd->nhwd", inputs, kernel, precision=lax.Precision.HIGHEST)


def kernel_grad(inputs, grad_z):
    return jnp.einsum("nhwc,nhwd->cd", inputs, grad_z, precision=lax.Precision.HIGHEST)


def masks(count_list, side_list):
    image = jnp.arange(side_list.shape[0])
    live = image % SLOTS < count_list[image // SLOTS]
    places = jnp.arange(MAP)
    inside = places[None, :] < side_list[:, None]
    keep = live[:, None, None] & inside[:, :, None] & inside[:, None, :]
    return keep.astype(jnp.float32)[..., None]


def local_sums(z, mask):
    return (jnp.sum(z * mask, axis=(0, 1, 2)), jnp.sum(z * z * mask, axis=(0, 1, 2)))


def finish(z, gain, shift, mask, first_sum, second_sum, total):
    mean = first_sum / total
    square = second_sum / total
    inverse_std = lax.rsqrt(square - mean * mean + epsilon)
    scaled = (z - mean) * inverse_std
    before = gain * scaled + shift
    return (mish(before) * mask, (scaled, inverse_std, before))


def norm_forward(z, gain, shift, mask, total):
    first_sum, second_sum = local_sums(z, mask)
    first_sum, second_sum = lax.psum((first_sum, second_sum), "bn")
    return finish(z, gain, shift, mask, first_sum, second_sum, total)


def norm_backward(grad_act, kept, gain, mask, total):
    scaled, inverse_std, before = kept
    unused, mish_pull = jax.vjp(mish, before)
    grad_before = mish_pull(grad_act * mask)[0]
    local_shift = jnp.sum(grad_before, axis=(0, 1, 2))
    local_gain = jnp.sum(grad_before * scaled, axis=(0, 1, 2))
    sum_shift, sum_gain = lax.psum((local_shift, local_gain), "bn")
    grad_z = mask * gain * inverse_std * (grad_before - (sum_shift + scaled * sum_gain) / total)
    return (grad_z, local_gain, local_shift)


def settle(kernel_part, gain_part, shift_part):
    return (kernel_part, gain_part, shift_part)


def local(
    features,
    image_counts,
    map_sides,
    split_kernel,
    split_gain,
    split_shift,
    inner_kernel,
    inner_gain,
    inner_shift,
    spread_kernel,
    spread_gain,
    spread_shift,
    transition_kernel,
    transition_gain,
    transition_shift,
    output_kernel,
    output_gain,
    output_shift,
    cotangent,
):
    half = inner_kernel.shape[0]
    split_weight = split_kernel.astype(jnp.float32)
    inner_weight = inner_kernel.astype(jnp.float32)
    spread_weight = spread_kernel.astype(jnp.float32)
    transition_weight = transition_kernel.astype(jnp.float32)
    output_weight = output_kernel.astype(jnp.float32)
    mask = masks(image_counts, map_sides)
    masked = features.astype(jnp.float32) * mask
    split_z = pointwise(masked, split_weight)
    first_sum, second_sum = local_sums(split_z, mask)
    first_sum, second_sum, total = lax.psum((first_sum, second_sum, jnp.sum(mask)), "bn")
    split, split_kept = finish(split_z, split_gain, split_shift, mask, first_sum, second_sum, total)
    part = split[..., :half]
    main = split[..., half:]
    inner, inner_kept = norm_forward(
        pointwise(main, inner_weight), inner_gain, inner_shift, mask, total
    )
    branch, spread_kept = norm_forward(
        convolve(inner, spread_weight), spread_gain, spread_shift, mask, total
    )
    joined = main + branch
    trans, trans_kept = norm_forward(
        pointwise(joined, transition_weight), transition_gain, transition_shift, mask, total
    )
    stacked = jnp.concatenate([trans, part], axis=-1)
    result, output_kept = norm_forward(
        pointwise(stacked, output_weight), output_gain, output_shift, mask, total
    )
    grad_z, gain_part, shift_part = norm_backward(cotangent, output_kept, output_gain, mask, total)
    grad_stacked = pointwise(grad_z, output_weight.T)
    output_grads = settle(kernel_grad(stacked, grad_z), gain_part, shift_part)
    grad_trans = grad_stacked[..., :half]
    grad_part = grad_stacked[..., half:]
    grad_z, gain_part, shift_part = norm_backward(
        grad_trans, trans_kept, transition_gain, mask, total
    )
    grad_joined = pointwise(grad_z, transition_weight.T)
    transition_grads = settle(kernel_grad(joined, grad_z), gain_part, shift_part)
    grad_z, gain_part, shift_part = norm_backward(
        grad_joined, spread_kept, spread_gain, mask, total
    )
    unused, spread_pull = jax.vjp(convolve, inner, spread_weight)
    grad_inner, grad_spread = spread_pull(grad_z)
    spread_grads = settle(grad_spread, gain_part, shift_part)
    grad_z, gain_part, shift_part = norm_backward(grad_inner, inner_kept, inner_gain, mask, total)
    grad_main = grad_joined + pointwise(grad_z, inner_weight.T)
    inner_grads = settle(kernel_grad(main, grad_z), gain_part, shift_part)
    grad_split = jnp.concatenate([grad_part, grad_main], axis=-1)
    grad_z, gain_part, shift_part = norm_backward(grad_split, split_kept, split_gain, mask, total)
    grad_features = pointwise(grad_z, split_weight.T) * mask
    split_grads = settle(kernel_grad(masked, grad_z), gain_part, shift_part)
    summed = lax.psum(
        (
            split_grads[0],
            split_grads[1],
            split_grads[2],
            inner_grads[0],
            inner_grads[1],
            inner_grads[2],
            spread_grads[0],
            spread_grads[1],
            spread_grads[2],
            transition_grads[0],
            transition_grads[1],
            transition_grads[2],
            output_grads[0],
            output_grads[1],
            output_grads[2],
        ),
        ("dp", "bn"),
    )
    return (
        result,
        grad_features,
        summed[0],
        summed[1],
        summed[2],
        summed[3],
        summed[4],
        summed[5],
        summed[6],
        summed[7],
        summed[8],
        summed[9],
        summed[10],
        summed[11],
        summed[12],
        summed[13],
        summed[14],
    )


def solution(mesh):
    return jax.shard_map(
        local,
        mesh=mesh,
        in_specs=(
            P(("dp", "bn"), None, None, None),
            P(("dp", "bn")),
            P(("dp", "bn")),
            P(),
            P(),
            P(),
            P(),
            P(),
            P(),
            P(),
            P(),
            P(),
            P(),
            P(),
            P(),
            P(),
            P(),
            P(),
            P(("dp", "bn"), None, None, None),
        ),
        out_specs=(
            P(("dp", "bn"), None, None, None),
            P(("dp", "bn"), None, None, None),
            P(),
            P(),
            P(),
            P(),
            P(),
            P(),
            P(),
            P(),
            P(),
            P(),
            P(),
            P(),
            P(),
            P(),
            P(),
        ),
        check_vma=False,
    )
```

profile of v0, /device:TPU:0, one launch (start us, length us, event | category | flops | bytes accessed | tf_op | source)
XLA Modules:
  0.0 992.0 jit_solution(5745738842142313879)
XLA Ops:
  9.7 19.9 %multiply_reduce_fusion.5 = (f32[1024]{0:T(1024)S(1)}, f32[1024]{0:T(1024)S(1)}, f32[4,19,19,1024]{3,2,1,0:T(8,128)}, f32[4,19,19,1024]{3,2,1,0:T(8,128)}) fusion(f32[4,19,19]{2,1,0:T(8,128)S(1)} %and_convert_fusion, bf16[4,19,19,1024]{3,0,2,1:T(4,128)(2,1)} %param.21, bf16[1024,1024]{1,0:T(8,128)(2,1)S(1)} %copy-done), kind=kOutput, calls=%fused_computation.52 | convolution fusion | flops 18183030784 | bytes 16897680 | tf_op jit(solution)/shard_map/nhwc,cd->nhwd/dot_general | solution.py:27
  29.6 9.3 all-reduce.11
  39.5 7.8 fusion.14
  76.0 43.0 %fusion.109 = (f32[19,32,3,512]{3,1,2,0:T(8,128)S(1)}, f32[19,32,3,512]{3,1,2,0:T(8,128)}) fusion(bf16[3,3,512,512]{3,2,1,0:T(8,128)(2,1)} %param.30, f32[19,4,8,5,512]{4,1,3,2,0:T(4,128)} %select_maximum_fusion.1, pred[32,3]{0,1:T(4,128)(4,1)S(1)} %copy-done.70), kind=kOutput, calls=%fused_computation.176 | convolution fusion | flops 49830199296 | bytes 18415712 | tf_op jit(solution)/shard_map/conv_general_dilated | solution.py:16
  155.1 7.8 fusion.23
  198.3 14.4 %multiply_reduce_fusion.3 = (f32[1024]{0:T(1024)S(1)}, f32[1024]{0:T(1024)S(1)}, f32[4,19,19,1024]{3,2,1,0:T(8,128)}) fusion(f32[4,19,19]{2,1,0:T(8,128)S(1)} %and_convert_fusion, bf16[1024,1024]{1,0:T(8,128)(2,1)S(1)} %copy-done.66, f32[4,19,19,512]{3,2,1,0:T(8,128)S(1)} %copy-done.16, f32[4,19,19,512]{3,2,1,0:T(8,128)S(1)} %fusion.55), kind=kOutput, calls=%fused_computation.47 | convolution fusion | flops 18178594816 | bytes 13940368 | tf_op jit(solution)/shard_map/nhwc,cd->nhwd/dot_general | solution.py:27
  220.1 17.3 %fusion.100 = (f32[1024]{0:T(1024)S(1)}, f32[1024]{0:T(1024)S(1)}, f32[4,19,19,1024]{3,2,1,0:T(8,128)}, f32[4,19,19,1024]{3,2,1,0:T(8,128)}) fusion(f32[1024]{0:T(1024)S(1)} %get-tuple-element.159, f32[4,19,19,1024]{3,2,1,0:T(8,128)} %get-tuple-element.175, f32[1024]{0:T(1024)S(1)} %get-tuple-element.158, f32[1024]{0:T(1024)S(1)} %copy-done.64, ...), kind=kLoop, calls=%fused_computation.172 | loop fusion | flops 42878976 | bytes 23688848 | tf_op jit(solution)/shard_map/reduce_sum | solution.py:66
  250.6 13.9 %fusion.72 = f32[4,19,19,1024]{3,2,1,0:T(8,128)} fusion(f32[4,19,19,1024]{3,2,1,0:T(8,128)S(1)} %subtract_multiply_fusion.1, bf16[1024,1024]{1,0:T(8,128)(2,1)S(1)} %copy-done.67), kind=kOutput, calls=%fused_computation.135 | convolution fusion | flops 18169724928 | bytes 13926400 | tf_op jit(solution)/shard_map/nhwc,cd->nhwd/dot_general | solution.py:27
  264.5 28.9 %fusion.64 = f32[1024,1024]{1,0:T(8,128)} fusion(f32[4,19,19,1024]{3,2,1,0:T(8,128)S(1)} %subtract_multiply_fusion.1, f32[4,19,19,512]{3,2,1,0:T(8,128)S(1)} %copy-done.17, f32[4,19,19,512]{3,2,1,0:T(8,128)S(1)} %copy-done.21), kind=kOutput, calls=%fused_computation.131 | convolution fusion | flops 18171203584 | bytes 16023552 | tf_op jit(solution)/shard_map/nhwc,nhwd->cd/dot_general | solution.py:31
  319.4 9.4 fusion.102
  335.4 18.8 %fusion.85 = f32[512,512]{1,0:T(8,128)} fusion(f32[4,19,19,512]{3,2,1,0:T(8,128)} %copy-done.6, f32[4,19,19,512]{3,2,1,0:T(8,128)} %get-tuple-element.147, f32[4,19,19,512]{3,2,1,0:T(8,128)} %get-tuple-element.174, f32[]{:T(128)} %get-tuple-element.142, f32[512]{0:T(512)S(1)} %get-tuple-element.129, f32[512]{0:T(512)S(1)} %get-tuple-element.130, ...), kind=kOutput, calls=%fused_computation.143 | convolution fusion | flops 4549085184 | bytes 9936532 | tf_op jit(solution)/shard_map/nhwc,nhwd->cd/dot_general | solution.py:31
  354.3 10.6 %fusion.40 = (f32[512]{0:T(512)S(1)}, f32[512]{0:T(512)S(1)}, f32[4,19,19,512]{3,2,1,0:T(8,128)}, f32[4,19,19,512]{3,2,1,0:T(8,128)}) fusion(f32[4,19,19]{2,1,0:T(8,128)S(1)} %and_convert_fusion, bf16[512,512]{1,0:T(8,128)(2,1)S(1)} %copy-done.27, f32[19,4,24,512]{3,2,1,0:T(8,128)S(1)} %copy-done.23, f32[19,4,24,512]{3,2,1,0:T(8,128)S(1)} %copy-done.24, ...), kind=kOutput, calls=%fused_computation.85 | convolution fusion | flops 4566088704 | bytes 21493764 | tf_op jit(solution)/shard_map/nhwc,cd->nhwd/dot_general | solution.py:27
  397.8 34.3 %broadcast_select_fusion = f32[19,32,3,512]{3,1,2,0:T(8,128)S(1)} fusion(pred[32,3]{0,1:T(4,128)(4,1)S(1)} %copy-done.70, bf16[3,3,512,512]{3,2,1,0:T(8,128)(2,1)} %param.30, f32[19,4,8,5,512]{4,1,3,2,0:T(4,128)} %select_maximum_fusion), kind=kOutput, calls=%fused_computation.140 | convolution fusion | flops 49829265408 | bytes 14680160 | tf_op jit(solution)/shard_map/transpose(jvp())/conv_general_dilated | solution.py:16
  444.1 8.4 fusion.101
  459.2 11.2 %convolution_add_fusion = f32[4,19,19,512]{3,2,1,0:T(8,128)} fusion(f32[4,19,19,512]{3,2,1,0:T(8,128)} %get-tuple-element.176, bf16[512,512]{1,0:T(8,128)(2,1)S(1)} %copy-done.69, f32[4,19,19,512]{3,2,1,0:T(8,128)} %get-tuple-element.145, f32[4,19,19,512]{3,2,1,0:T(8,128)} %get-tuple-element.171, f32[512]{0:T(512)S(1)} %get-tuple-element.125, ...), kind=kOutput, calls=%fused_computation.139 | convolution fusion | flops 4549824512 | bytes 12369556 | tf_op jit(solution)/shard_map/nhwc,cd->nhwd/dot_general | solution.py:27
  470.4 10.2 %fusion.80 = f32[512,512]{1,0:T(8,128)} fusion(f32[4,19,19,512]{3,2,1,0:T(8,128)S(1)} %copy-done.15, f32[4,19,19,512]{3,2,1,0:T(8,128)S(1)} %copy-done.22, f32[4,19,19,512]{3,2,1,0:T(8,128)S(1)} %copy-done.2, f32[512]{0:T(512)S(1)} %get-tuple-element.125, f32[512]{0:T(512)S(1)} %get-tuple-element.126, f32[]{:T(128)} %get-tuple-element.142, ...), kind=kOutput, calls=%fused_computation.142 | convolution fusion | flops 4549085184 | bytes 9936532 | tf_op jit(solution)/shard_map/nhwc,nhwd->cd/dot_general | solution.py:31
  480.7 108.9 %fusion.56 = f32[3,3,512,512]{3,2,1,0:T(8,128)} fusion(f32[4,19,19,512]{3,2,1,0:T(8,128)S(1)} %copy-done.9, f32[4,19,19,512]{3,2,1,0:T(8,128)S(1)} %copy-done.19), kind=kOutput, calls=%fused_computation.127 | convolution fusion | flops 38063308800 | bytes 15351808 | tf_op jit(solution)/shard_map/transpose(jvp())/conv_general_dilated | solution.py:16
  589.7 12.9 %fusion.99 = (f32[1024]{0:T(1024)S(1)}, f32[1024]{0:T(1024)S(1)}, f32[4,19,19,1024]{3,2,1,0:T(8,128)}) fusion(f32[1024]{0:T(1024)S(1)} %copy-done.31, f32[4,19,19,1024]{3,2,1,0:T(8,128)} %get-tuple-element.170, f32[1024]{0:T(1024)S(1)} %copy-done.29, f32[1024]{0:T(1024)S(1)} %copy-done.55, f32[1024]{0:T(1024)S(1)} %copy-done.37, ...), kind=kLoop, calls=%fused_computation.171 | loop fusion | flops 41400320 | bytes 17774224 | tf_op jit(solution)/shard_map/reduce_sum | solution.py:66
  608.3 7.4 subtract_multiply_fusion
  618.7 28.9 %fusion.59 = f32[1024,1024]{1,0:T(8,128)} fusion(f32[4,19,19,1024]{3,2,1,0:T(8,128)S(1)} %subtract_multiply_fusion, f32[4,19,19,1024]{3,2,1,0:T(8,128)S(1)} %copy-done.71), kind=kOutput, calls=%fused_computation.130 | convolution fusion | flops 18169724928 | bytes 16023552 | tf_op jit(solution)/shard_map/nhwc,nhwd->cd/dot_general | solution.py:31
  647.7 10.0 %copy.115 = f32[4,19,19,1024]{3,0,2,1:T(4,128)} copy(f32[4,19,19,1024]{3,2,1,0:T(8,128)} %get-tuple-element.152) | data formatting | bytes 11829248
  657.7 14.8 %broadcast_multiply_fusion = f32[4,19,19,1024]{3,2,1,0:T(8,128)S(1)} fusion(f32[4,19,19]{2,1,0:T(8,128)S(1)} %copy-done.11, f32[4,19,19,1024]{3,2,1,0:T(8,128)} %copy-done.13, bf16[1024,1024]{1,0:T(8,128)(2,1)S(1)} %copy-done), kind=kOutput, calls=%fused_computation.126 | convolution fusion | flops 18171203584 | bytes 13932176 | tf_op jit(solution)/shard_map/nhwc,cd->nhwd/dot_general | solution.py:27
  679.6 42.0 %all-reduce = (f32[1024]{0:T(1024)}, f32[1024]{0:T(1024)}, f32[512]{0:T(512)}, f32[512]{0:T(512)}, f32[512]{0:T(512)}, /*index=5*/f32[512]{0:T(512)}, f32[512]{0...) all-reduce(f32[1024]{0:T(1024)S(1)} %get-tuple-element.93, ...), channel_id=1, replica_groups=mesh['dp'=8,'bn'=4] {'dp','bn'}, use_global_device_ids=true, to_apply=%region_43.46 | all-reduce | flops 7168 | bytes 57344 | tf_op jit(solution)/shard_map/psum | solution.py:149
  721.6 247.1 %all-reduce.14.cloned.1.call-done = (f32[1024,1024]{1,0:T(8,128)}, f32[512,512]{1,0:T(8,128)}, f32[3,3,512,512]{3,2,1,0:T(8,128)}, f32[512,512]{1,0:T(8,128)}, f32[1024,1024]{1,0:T(8,128)}) async-done(((f32[1024,1024]{1,0:T(8,128)}, f32[512,512]{1,0:T(8,128)}, f32[3,3,512,512]{3,2,1,0:T(8,128)}, f32[512,512]{1,0:T(8,128)}, f32[1024,1024]{1,0:T(8,128)}), (f32[1024,1024]{1,0:T(8,128)}, f32[512,512]{1,0:T(8,128)}, ...) | async-done | bytes 19922960 | tf_op jit(solution)/shard_map/psum | solution.py:149
  (203 shorter events, 238.4 us)
Async XLA Ops:
  7.2 961.4 %all-reduce.14.cloned.1.call-start = ((), (), s32[]{:S(2)}) async-start(), calls=%async_computation | async-start | bytes 39845888 | tf_op jit(solution)/shard_map/psum | solution.py:149
  9.0 461.4 %copy-start.10 = (f32[4,19,19]{2,1,0:T(8,128)}, f32[4,19,19]{2,1,0:T(8,128)S(1)}, u32[]{:S(2)}) copy-start(f32[4,19,19]{2,1,0:T(8,128)S(1)} %and_convert_fusion) | copy-start | bytes 17332
  9.7 29.8 %copy-start.36 = (f32[1024]{0:T(1024)S(1)}, f32[1024]{0:T(1024)}, u32[]{:S(2)}) copy-start(f32[1024]{0:T(1024)} %param.25) | copy-start | bytes 12292
  9.7 29.8 %copy-start.54 = (f32[1024]{0:T(1024)S(1)}, f32[1024]{0:T(1024)}, u32[]{:S(2)}) copy-start(f32[1024]{0:T(1024)} %param.26) | copy-start | bytes 12292
  198.3 14.4 %copy-start.20 = (f32[4,19,19,512]{3,2,1,0:T(8,128)}, f32[4,19,19,512]{3,2,1,0:T(8,128)S(1)}, u32[]{:S(2)}) copy-start(f32[4,19,19,512]{3,2,1,0:T(8,128)S(1)} %fusion.55) | copy-start | bytes 8871940
  198.3 21.8 %copy-start.56 = (f32[1024]{0:T(1024)S(1)}, f32[1024]{0:T(1024)}, u32[]{:S(2)}) copy-start(f32[1024]{0:T(1024)} %param.37) | copy-start | bytes 12292
  198.3 21.8 %copy-start.64 = (f32[1024]{0:T(1024)S(1)}, f32[1024]{0:T(1024)}, u32[]{:S(2)}) copy-start(f32[1024]{0:T(1024)} %param.38) | copy-start | bytes 12292
  264.5 28.9 %copy-start.3 = (f32[19,32,3,512]{3,1,2,0:T(8,128)S(1)}, f32[19,32,3,512]{3,1,2,0:T(8,128)}, u32[]{:S(2)}) copy-start(f32[19,32,3,512]{3,1,2,0:T(8,128)} %get-tuple-element.151) | copy-start | bytes 11206660
  328.8 25.4 %copy-start.46 = (f32[512]{0:T(512)}, f32[512]{0:T(512)S(1)}, u32[]{:S(2)}) copy-start(f32[512]{0:T(512)S(1)} %get-tuple-element.104) | copy-start | bytes 6148
  328.8 25.4 %copy-start.48 = (f32[512]{0:T(512)}, f32[512]{0:T(512)S(1)}, u32[]{:S(2)}) copy-start(f32[512]{0:T(512)S(1)} %get-tuple-element.105) | copy-start | bytes 6148
  335.4 18.8 %copy-start.4 = (f32[4,19,19,512]{3,2,1,0:T(8,128)S(1)}, f32[4,19,19,512]{3,2,1,0:T(8,128)}, u32[]{:S(2)}) copy-start(f32[4,19,19,512]{3,2,1,0:T(8,128)} %get-tuple-element.174) | copy-start | bytes 8871940
  335.4 18.8 %copy-start.23 = (f32[19,4,24,512]{3,2,1,0:T(8,128)S(1)}, f32[19,4,24,512]{3,2,1,0:T(8,128)}, u32[]{:S(2)}) copy-start(f32[19,4,24,512]{3,2,1,0:T(8,128)} %reshape.156) | copy-start | bytes 11206660
  335.4 18.8 %copy-start.24 = (f32[19,4,24,512]{3,2,1,0:T(8,128)S(1)}, f32[19,4,24,512]{3,2,1,0:T(8,128)}, u32[]{:S(2)}) copy-start(f32[19,4,24,512]{3,2,1,0:T(8,128)} %reshape.145) | copy-start | bytes 11206660
  335.4 18.8 %copy-start.25 = (f32[4,19,19,512]{3,2,1,0:T(8,128)S(1)}, f32[4,19,19,512]{3,2,1,0:T(8,128)}, u32[]{:S(2)}) copy-start(f32[4,19,19,512]{3,2,1,0:T(8,128)} %get-tuple-element.147) | copy-start | bytes 8871940
  444.1 15.0 %copy-start.69 = (bf16[512,512]{1,0:T(8,128)(2,1)S(1)}, bf16[512,512]{1,0:T(8,128)(2,1)}, u32[]{:S(2)}) copy-start(bf16[512,512]{1,0:T(8,128)(2,1)} %param.27) | copy-start | bytes 1572868
  452.5 17.8 %copy-start.50 = (f32[512]{0:T(512)}, f32[512]{0:T(512)S(1)}, u32[]{:S(2)}) copy-start(f32[512]{0:T(512)S(1)} %get-tuple-element.100) | copy-start | bytes 6148
  452.5 17.8 %copy-start.52 = (f32[512]{0:T(512)}, f32[512]{0:T(512)S(1)}, u32[]{:S(2)}) copy-start(f32[512]{0:T(512)S(1)} %get-tuple-element.101) | copy-start | bytes 6148
  480.6 109.0 %copy-start.7 = (f32[4,19,19,512]{3,2,1,0:T(8,128)S(1)}, f32[4,19,19,512]{3,2,1,0:T(8,128)}, u32[]{:S(2)}) copy-start(f32[4,19,19,512]{3,2,1,0:T(8,128)} %get-tuple-element.156) | copy-start | bytes 8871940
  480.6 109.0 %copy-start.11 = (f32[4,19,19]{2,1,0:T(8,128)S(1)}, f32[4,19,19]{2,1,0:T(8,128)}, u32[]{:S(2)}) copy-start(f32[4,19,19]{2,1,0:T(8,128)} %copy-done.10) | copy-start | bytes 17332
  480.6 109.0 %copy-start.18 = (f32[4,19,19,512]{3,2,1,0:T(8,128)S(1)}, f32[4,19,19,512]{3,2,1,0:T(8,128)}, u32[]{:S(2)}) copy-start(f32[4,19,19,512]{3,2,1,0:T(8,128)} %convolution_add_fusion) | copy-start | bytes 8871940
  480.6 109.0 %copy-start.29 = (f32[1024]{0:T(1024)S(1)}, f32[1024]{0:T(1024)}, u32[]{:S(2)}) copy-start(f32[1024]{0:T(1024)} %copy-done.28) | copy-start | bytes 12292
  480.6 109.0 %copy-start.31 = (f32[1024]{0:T(1024)S(1)}, f32[1024]{0:T(1024)}, u32[]{:S(2)}) copy-start(f32[1024]{0:T(1024)} %copy-done.30) | copy-start | bytes 12292
  480.6 109.0 %copy-start.37 = (f32[1024]{0:T(1024)S(1)}, f32[1024]{0:T(1024)}, u32[]{:S(2)}) copy-start(f32[1024]{0:T(1024)} %param.25) | copy-start | bytes 12292
  480.6 109.0 %copy-start.55 = (f32[1024]{0:T(1024)S(1)}, f32[1024]{0:T(1024)}, u32[]{:S(2)}) copy-start(f32[1024]{0:T(1024)} %param.26) | copy-start | bytes 12292
  (49 other events, 392.1 us)
Sparse Core Ops, SparseCore 0:
  647.8 320.8 all-reduce.13
where the time goes:
time: 998 us; the launch traced here: 992 us
  matrix products  369 us (37%)
  waiting for transfers between devices  247 us (25%)
  local copies, waits for them, and re-layouts  131 us (13%)
  other arithmetic  122 us (12%)
  blocking collectives  107 us (11%)
  between operations  16.3 us (2%)
    psum x1, waiting for transfers between devices, local(): lax.psum((split_grads[0], split_grads[1], split_grads[2], inner_grads[0],...  247 us
    conv_general_dilated x3, matrix products, convolve(): lax.conv_general_dilated(inputs, kernel, (1, 1), ((1, 1), (1, 1)), dimens...  186 us
    dot_general x8, matrix products, pointwise(): jnp.einsum('nhwc,cd->nhwd', inputs, kernel, precision=lax.Precision.HIGHEST)  95.4 us
    dot_general x4, matrix products, kernel_grad(): jnp.einsum('nhwc,nhwd->cd', inputs, grad_z, precision=lax.Precision.HIGHEST)  86.9 us
    reduce_sum x4, other arithmetic, norm_backward(): local_shift = jnp.sum(grad_before, axis=(0, 1, 2))  48 us
    psum x1, blocking collectives, local(): lax.psum((split_grads[0], split_grads[1], split_grads[2], inner_grads[0],...  42 us
    unnamed x153, local copies, waits for them, and re-layouts  40.6 us
    psum x5, blocking collectives, norm_backward(): sum_shift, sum_gain = lax.psum((local_shift, local_gain), 'bn')  30.5 us
  transfers between devices with their start and end apart: 1, of which 1 were waited for; matrix products, arithmetic and copies ran while one was open for 3% of the time, Pallas kernels for 0%

commit v1 on v0

--- a/solution.py
+++ b/solution.py
@@ -147,24 +147,27 @@
     grad_features = pointwise(grad_z, split_weight.T) * mask
     split_grads = settle(kernel_grad(masked, grad_z), gain_part, shift_part)
     summed = lax.psum(
-        (
-            split_grads[0],
-            split_grads[1],
-            split_grads[2],
-            inner_grads[0],
-            inner_grads[1],
-            inner_grads[2],
-            spread_grads[0],
-            spread_grads[1],
-            spread_grads[2],
-            transition_grads[0],
-            transition_grads[1],
-            transition_grads[2],
-            output_grads[0],
-            output_grads[1],
-            output_grads[2],
+        lax.psum(
+            (
+                split_grads[0],
+                split_grads[1],
+                split_grads[2],
+                inner_grads[0],
+                inner_grads[1],
+                inner_grads[2],
+                spread_grads[0],
+                spread_grads[1],
+                spread_grads[2],
+                transition_grads[0],
+                transition_grads[1],
+                transition_grads[2],
+                output_grads[0],
+                output_grads[1],
+                output_grads[2],
+            ),
+            "bn",
         ),
-        ("dp", "bn"),
+        "dp",
     )
     return (
         result,

time: 998 us -> 1630 us (1.63)
  waiting for transfers between devices: 247 us -> 878 us
    psum x0 -> x1, waiting for transfers between devices: none -> 536 us  [local(): lax.psum(lax.psum((split_grads[0], split_grads[1], split_grads[2], inner_...]
    psum x1, waiting for transfers between devices: 247 us -> 342 us  [local(): lax.psum((split_grads[0], split_grads[1], split_grads[2], inner_grads[0],...]
  transfers between devices with their start and end apart: 1 -> 2, of which waited for: 1 -> 2; matrix products, arithmetic and copies ran while one was open for 3% -> 2% of each run, Pallas kernels for 0% -> 0%
where the time goes in v1:
time: 1630 us; the launch traced here: 1620 us
  waiting for transfers between devices  878 us (54%)
  matrix products  370 us (23%)
  local copies, waits for them, and re-layouts  131 us (8%)
  other arithmetic  123 us (8%)
  blocking collectives  105 us (6%)
  between operations  16.3 us (1%)
    psum x1, waiting for transfers between devices, local(): lax.psum(lax.psum((split_grads[0], split_grads[1], split_grads[2], inner_...  536 us
    psum x1, waiting for transfers between devices, local(): lax.psum((split_grads[0], split_grads[1], split_grads[2], inner_grads[0],...  342 us
    conv_general_dilated x3, matrix products, convolve(): lax.conv_general_dilated(inputs, kernel, (1, 1), ((1, 1), (1, 1)), dimens...  186 us
    dot_general x8, matrix products, pointwise(): jnp.einsum('nhwc,cd->nhwd', inputs, kernel, precision=lax.Precision.HIGHEST)  96.4 us
    dot_general x4, matrix products, kernel_grad(): jnp.einsum('nhwc,nhwd->cd', inputs, grad_z, precision=lax.Precision.HIGHEST)  87 us
    reduce_sum x4, other arithmetic, norm_backward(): local_shift = jnp.sum(grad_before, axis=(0, 1, 2))  47.9 us
    unnamed x153, local copies, waits for them, and re-layouts  40.5 us
    psum x1, blocking collectives, local(): lax.psum(lax.psum((split_grads[0], split_grads[1], split_grads[2], inner_...  40.3 us
  transfers between devices with their start and end apart: 2, of which 2 were waited for; matrix products, arithmetic and copies ran while one was open for 2% of the time, Pallas kernels for 0%

profile of v1, /device:TPU:0, one launch (start us, length us, event | category | flops | bytes accessed | tf_op | source)
XLA Modules:
  0.0 1622.4 jit_solution(16651037444953404785)
XLA Ops:
  9.7 19.9 %multiply_reduce_fusion.5 = (f32[1024]{0:T(1024)S(1)}, f32[1024]{0:T(1024)S(1)}, f32[4,19,19,1024]{3,2,1,0:T(8,128)}, f32[4,19,19,1024]{3,2,1,0:T(8,128)}) fusion(f32[4,19,19]{2,1,0:T(8,128)S(1)} %and_convert_fusion, bf16[4,19,19,1024]{3,0,2,1:T(4,128)(2,1)} %param.21, bf16[1024,1024]{1,0:T(8,128)(2,1)S(1)} %copy-done), kind=kOutput, calls=%fused_computation.52 | convolution fusion | flops 18183030784 | bytes 16897680 | tf_op jit(solution)/shard_map/nhwc,cd->nhwd/dot_general | solution.py:27
  29.6 9.4 all-reduce.11
  39.6 7.8 fusion.14
  76.5 43.0 %fusion.109 = (f32[19,32,3,512]{3,1,2,0:T(8,128)S(1)}, f32[19,32,3,512]{3,1,2,0:T(8,128)}) fusion(bf16[3,3,512,512]{3,2,1,0:T(8,128)(2,1)} %param.30, f32[19,4,8,5,512]{4,1,3,2,0:T(4,128)} %select_maximum_fusion.1, pred[32,3]{0,1:T(4,128)(4,1)S(1)} %copy-done.70), kind=kOutput, calls=%fused_computation.176 | convolution fusion | flops 49830199296 | bytes 18415712 | tf_op jit(solution)/shard_map/conv_general_dilated | solution.py:16
  155.6 7.8 fusion.23
  198.9 14.4 multiply_reduce_fusion.3
  220.7 17.2 %fusion.100 = (f32[1024]{0:T(1024)S(1)}, f32[1024]{0:T(1024)S(1)}, f32[4,19,19,1024]{3,2,1,0:T(8,128)}, f32[4,19,19,1024]{3,2,1,0:T(8,128)}) fusion(f32[1024]{0:T(1024)S(1)} %get-tuple-element.164, f32[4,19,19,1024]{3,2,1,0:T(8,128)} %get-tuple-element.180, f32[1024]{0:T(1024)S(1)} %get-tuple-element.163, f32[1024]{0:T(1024)S(1)} %copy-done.56, ...), kind=kLoop, calls=%fused_computation.172 | loop fusion | flops 42878976 | bytes 23688848 | tf_op jit(solution)/shard_map/reduce_sum | solution.py:66
  251.2 13.9 fusion.72
  265.1 28.9 %fusion.64 = f32[1024,1024]{1,0:T(8,128)} fusion(f32[4,19,19,1024]{3,2,1,0:T(8,128)S(1)} %subtract_multiply_fusion.1, f32[4,19,19,512]{3,2,1,0:T(8,128)S(1)} %copy-done.17, f32[4,19,19,512]{3,2,1,0:T(8,128)S(1)} %copy-done.21), kind=kOutput, calls=%fused_computation.131 | convolution fusion | flops 18171203584 | bytes 16023552 | tf_op jit(solution)/shard_map/nhwc,nhwd->cd/dot_general | solution.py:31
  319.9 9.4 fusion.102
  336.0 18.9 %fusion.85 = f32[512,512]{1,0:T(8,128)} fusion(f32[4,19,19,512]{3,2,1,0:T(8,128)} %copy-done.6, f32[4,19,19,512]{3,2,1,0:T(8,128)} %get-tuple-element.152, f32[4,19,19,512]{3,2,1,0:T(8,128)} %get-tuple-element.179, f32[]{:T(128)} %get-tuple-element.142, f32[512]{0:T(512)S(1)} %get-tuple-element.129, f32[512]{0:T(512)S(1)} %get-tuple-element.130, ...), kind=kOutput, calls=%fused_computation.143 | convolution fusion | flops 4549085184 | bytes 9936532 | tf_op jit(solution)/shard_map/nhwc,nhwd->cd/dot_general | solution.py:31
  354.9 10.6 fusion.40
  398.5 34.3 %broadcast_select_fusion = f32[19,32,3,512]{3,1,2,0:T(8,128)S(1)} fusion(pred[32,3]{0,1:T(4,128)(4,1)S(1)} %copy-done.70, bf16[3,3,512,512]{3,2,1,0:T(8,128)(2,1)} %param.30, f32[19,4,8,5,512]{4,1,3,2,0:T(4,128)} %select_maximum_fusion), kind=kOutput, calls=%fused_computation.140 | convolution fusion | flops 49829265408 | bytes 14680160 | tf_op jit(solution)/shard_map/transpose(jvp())/conv_general_dilated | solution.py:16
  444.8 8.4 fusion.101
  459.9 11.3 convolution_add_fusion
  471.2 10.2 fusion.80
  481.5 108.9 %fusion.56 = f32[3,3,512,512]{3,2,1,0:T(8,128)} fusion(f32[4,19,19,512]{3,2,1,0:T(8,128)S(1)} %copy-done.9, f32[4,19,19,512]{3,2,1,0:T(8,128)S(1)} %copy-done.19), kind=kOutput, calls=%fused_computation.127 | convolution fusion | flops 38063308800 | bytes 15351808 | tf_op jit(solution)/shard_map/transpose(jvp())/conv_general_dilated | solution.py:16
  590.6 12.8 fusion.99
  619.5 28.9 %fusion.59 = f32[1024,1024]{1,0:T(8,128)} fusion(f32[4,19,19,1024]{3,2,1,0:T(8,128)S(1)} %subtract_multiply_fusion, f32[4,19,19,1024]{3,2,1,0:T(8,128)S(1)} %copy-done.71), kind=kOutput, calls=%fused_computation.130 | convolution fusion | flops 18169724928 | bytes 16023552 | tf_op jit(solution)/shard_map/nhwc,nhwd->cd/dot_general | solution.py:31
  648.6 341.7 %all-reduce.18.cloned.1.call-done = (f32[1024,1024]{1,0:T(8,128)}, f32[512,512]{1,0:T(8,128)}, f32[3,3,512,512]{3,2,1,0:T(8,128)}, f32[512,512]{1,0:T(8,128)}, f32[1024,1024]{1,0:T(8,128)}) async-done(((f32[1024,1024]{1,0:T(8,128)}, f32[512,512]{1,0:T(8,128)}, f32[3,3,512,512]{3,2,1,0:T(8,128)}, f32[512,512]{1,0:T(8,128)}, f32[1024,1024]{1,0:T(8,128)}), (f32[1024,1024]{1,0:T(8,128)}, f32[512,512]{1,0:T(8,128)}, ...) | async-done | bytes 19922960 | tf_op jit(solution)/shard_map/psum | solution.py:150
  990.3 10.0 copy.115
  1000.4 15.6 broadcast_multiply_fusion
  1023.0 40.3 %all-reduce = (f32[1024]{0:T(1024)}, f32[1024]{0:T(1024)}, f32[512]{0:T(512)}, f32[512]{0:T(512)}, f32[512]{0:T(512)}, /*index=5*/f32[512]{0:T(512)}, f32[512]{0...) all-reduce(f32[1024]{0:T(1024)S(1)} %get-tuple-element.123, ...), channel_id=1, replica_groups=mesh['dp'=8,'bn'=4] {'dp'}, use_global_device_ids=true, to_apply=%region_44.47 | all-reduce | flops 7168 | bytes 57344 | tf_op jit(solution)/shard_map/psum | solution.py:149
  1063.2 535.9 %all-reduce.16.cloned.1.call-done = (f32[1024,1024]{1,0:T(8,128)}, f32[512,512]{1,0:T(8,128)}, f32[3,3,512,512]{3,2,1,0:T(8,128)}, f32[512,512]{1,0:T(8,128)}, f32[1024,1024]{1,0:T(8,128)}) async-done(((f32[1024,1024]{1,0:T(8,128)}, f32[512,512]{1,0:T(8,128)}, f32[3,3,512,512]{3,2,1,0:T(8,128)}, f32[512,512]{1,0:T(8,128)}, f32[1024,1024]{1,0:T(8,128)}), (f32[1024,1024]{1,0:T(8,128)}, f32[512,512]{1,0:T(8,128)}, ...) | async-done | bytes 19922960 | tf_op jit(solution)/shard_map/psum | solution.py:149
  (206 shorter events, 246.4 us)
Async XLA Ops:
  7.2 983.1 %all-reduce.18.cloned.1.call-start = ((), (), s32[]{:S(2)}) async-start(), calls=%async_computation.1 | async-start | bytes 39845888 | tf_op jit(solution)/shard_map/psum | solution.py:150
  9.0 462.2 %copy-start.10 = (f32[4,19,19]{2,1,0:T(8,128)}, f32[4,19,19]{2,1,0:T(8,128)S(1)}, u32[]{:S(2)}) copy-start(f32[4,19,19]{2,1,0:T(8,128)S(1)} %and_convert_fusion) | copy-start | bytes 17332
  9.7 29.9 %copy-start.32 = (f32[1024]{0:T(1024)S(1)}, f32[1024]{0:T(1024)}, u32[]{:S(2)}) copy-start(f32[1024]{0:T(1024)} %param.25) | copy-start | bytes 12292
  9.7 29.9 %copy-start.42 = (f32[1024]{0:T(1024)S(1)}, f32[1024]{0:T(1024)}, u32[]{:S(2)}) copy-start(f32[1024]{0:T(1024)} %param.26) | copy-start | bytes 12292
  198.9 14.4 copy-start.20
  198.9 21.8 %copy-start.44 = (f32[1024]{0:T(1024)S(1)}, f32[1024]{0:T(1024)}, u32[]{:S(2)}) copy-start(f32[1024]{0:T(1024)} %param.37) | copy-start | bytes 12292
  198.9 21.8 %copy-start.56 = (f32[1024]{0:T(1024)S(1)}, f32[1024]{0:T(1024)}, u32[]{:S(2)}) copy-start(f32[1024]{0:T(1024)} %param.38) | copy-start | bytes 12292
  251.1 13.9 copy-start.17
  265.1 28.9 %copy-start.3 = (f32[19,32,3,512]{3,1,2,0:T(8,128)S(1)}, f32[19,32,3,512]{3,1,2,0:T(8,128)}, u32[]{:S(2)}) copy-start(f32[19,32,3,512]{3,1,2,0:T(8,128)} %get-tuple-element.156) | copy-start | bytes 11206660
  335.9 18.9 %copy-start.58 = (f32[512]{0:T(512)}, f32[512]{0:T(512)S(1)}, u32[]{:S(2)}) copy-start(f32[512]{0:T(512)S(1)} %get-tuple-element.129) | copy-start | bytes 6148
  335.9 18.9 %copy-start.60 = (f32[512]{0:T(512)}, f32[512]{0:T(512)S(1)}, u32[]{:S(2)}) copy-start(f32[512]{0:T(512)S(1)} %get-tuple-element.130) | copy-start | bytes 6148
  335.9 18.9 %copy-start.4 = (f32[4,19,19,512]{3,2,1,0:T(8,128)S(1)}, f32[4,19,19,512]{3,2,1,0:T(8,128)}, u32[]{:S(2)}) copy-start(f32[4,19,19,512]{3,2,1,0:T(8,128)} %get-tuple-element.179) | copy-start | bytes 8871940
  335.9 18.9 %copy-start.23 = (f32[19,4,24,512]{3,2,1,0:T(8,128)S(1)}, f32[19,4,24,512]{3,2,1,0:T(8,128)}, u32[]{:S(2)}) copy-start(f32[19,4,24,512]{3,2,1,0:T(8,128)} %reshape.156) | copy-start | bytes 11206660
  335.9 18.9 %copy-start.24 = (f32[19,4,24,512]{3,2,1,0:T(8,128)S(1)}, f32[19,4,24,512]{3,2,1,0:T(8,128)}, u32[]{:S(2)}) copy-start(f32[19,4,24,512]{3,2,1,0:T(8,128)} %reshape.145) | copy-start | bytes 11206660
  335.9 18.9 %copy-start.25 = (f32[4,19,19,512]{3,2,1,0:T(8,128)S(1)}, f32[4,19,19,512]{3,2,1,0:T(8,128)}, u32[]{:S(2)}) copy-start(f32[4,19,19,512]{3,2,1,0:T(8,128)} %get-tuple-element.152) | copy-start | bytes 8871940
  444.8 15.0 copy-start.69
  481.5 109.0 %copy-start.7 = (f32[4,19,19,512]{3,2,1,0:T(8,128)S(1)}, f32[4,19,19,512]{3,2,1,0:T(8,128)}, u32[]{:S(2)}) copy-start(f32[4,19,19,512]{3,2,1,0:T(8,128)} %get-tuple-element.161) | copy-start | bytes 8871940
  481.5 109.0 %copy-start.11 = (f32[4,19,19]{2,1,0:T(8,128)S(1)}, f32[4,19,19]{2,1,0:T(8,128)}, u32[]{:S(2)}) copy-start(f32[4,19,19]{2,1,0:T(8,128)} %copy-done.10) | copy-start | bytes 17332
  481.5 109.0 %copy-start.18 = (f32[4,19,19,512]{3,2,1,0:T(8,128)S(1)}, f32[4,19,19,512]{3,2,1,0:T(8,128)}, u32[]{:S(2)}) copy-start(f32[4,19,19,512]{3,2,1,0:T(8,128)} %convolution_add_fusion) | copy-start | bytes 8871940
  481.5 109.0 %copy-start.29 = (f32[1024]{0:T(1024)S(1)}, f32[1024]{0:T(1024)}, u32[]{:S(2)}) copy-start(f32[1024]{0:T(1024)} %copy-done.28) | copy-start | bytes 12292
  481.5 109.0 %copy-start.31 = (f32[1024]{0:T(1024)S(1)}, f32[1024]{0:T(1024)}, u32[]{:S(2)}) copy-start(f32[1024]{0:T(1024)} %copy-done.30) | copy-start | bytes 12292
  481.5 109.0 %copy-start.33 = (f32[1024]{0:T(1024)S(1)}, f32[1024]{0:T(1024)}, u32[]{:S(2)}) copy-start(f32[1024]{0:T(1024)} %param.25) | copy-start | bytes 12292
  481.5 109.0 %copy-start.43 = (f32[1024]{0:T(1024)S(1)}, f32[1024]{0:T(1024)}, u32[]{:S(2)}) copy-start(f32[1024]{0:T(1024)} %param.26) | copy-start | bytes 12292
  648.5 950.6 %all-reduce.16.cloned.1.call-start = ((), (), s32[]{:S(2)}) async-start(), calls=%async_computation | async-start | bytes 39845888 | tf_op jit(solution)/shard_map/psum | solution.py:149
  (50 other events, 379.5 us)
Sparse Core Ops, SparseCore 0:
  648.6 341.6 all-reduce.17
  995.5 603.6 all-reduce.15
